TPU v7x, 256 devices: a whole 4x4x8 slice. The times are simulated.
256 devices in a mesh: row: 16 (over y_lo, x, core), col: 16 (over y_hi, z).
Axes of the slice: x: 4, y: 4 (y_hi: 2, y_lo: 2; y = y_hi * 2 + y_lo), z: 8, core: 2. Of those that a mesh axis runs over, the one named last changes fastest.
Arguments:
- field: bfloat16 [64, 64, 32, 512], P('row', 'col'), may hold values from -6 to 6
- near_kernel: bfloat16 [9, 2, 2, 256, 256], replicated, may hold values from -0.09375 to 0.09375
- contact: int32 [64, 64, 9], P('row', 'col'), may hold values from 0 to 1
- pillar_shift: int32 [64, 64, 2], P('row', 'col'), may hold values from 0 to 15
- wave_index: int32 [2048, 2], replicated, may hold values from -32 to 31
- wave_form: bfloat16 [2048, 2, 256], replicated, may hold values from -0.25 to 0.25
- wave_weight: float32 [2048], replicated, may hold values from 0.5 to 4
Outputs:
- applied: float32 [64, 64, 32, 512], P('row', 'col')
All inputs are finite; a program needn't handle non-finite values.
Results may differ from a plain program's by a relative error of at most 0.0038.
Values may be sent and summed in bfloat16 or wider, within the bound.
A program may use at most 128 MiB of HBM per device.

v0:
```python
import math
import jax
import jax.numpy as jnp
from jax import lax
from jax.sharding import PartitionSpec as P

Q = 16
bloch_row = 0.3
bloch_col = 0.17


def extended(cells, sides, width):
    for axis, dim in sides:
        count = lax.axis_size(axis)
        head = lax.slice_in_dim(cells, 0, width, axis=dim)
        tail = lax.slice_in_dim(cells, cells.shape[dim] - width, cells.shape[dim], axis=dim)
        cells = jnp.concatenate(
            [
                lax.ppermute(tail, axis, [(i, (i + 1) % count) for i in range(count)]),
                cells,
                lax.ppermute(head, axis, [((i + 1) % count, i) for i in range(count)]),
            ],
            axis=dim,
        )
    return cells


def realify(real_part, imag_part):
    upper = jnp.concatenate([real_part.T, imag_part.T], axis=1)
    lower = jnp.concatenate([-imag_part.T, real_part.T], axis=1)
    return jnp.concatenate([upper, lower], axis=0)


def wave_angle(wave_index, fine_row, fine_col, row_mod, col_mod):
    order_row = wave_index[:, 0:1]
    order_col = wave_index[:, 1:2]
    turn_row = jnp.mod(order_row * fine_row[None, :], row_mod).astype(jnp.float32) / row_mod
    turn_col = jnp.mod(order_col * fine_col[None, :], col_mod).astype(jnp.float32) / col_mod
    drift = (
        bloch_row * fine_row.astype(jnp.float32) / row_mod
        + bloch_col * fine_col.astype(jnp.float32) / col_mod
    )
    return 2.0 * math.pi * (turn_row + turn_col + drift[None, :])


def local(field, near_kernel, contact, pillar_shift, wave_index, wave_form, wave_weight):
    rows_here = field.shape[0]
    cols_here = field.shape[1]
    sources = field.shape[2]
    width = field.shape[3]
    waves = wave_form.shape[0]
    n_row = lax.axis_size("row")
    n_col = lax.axis_size("col")
    rows_total = rows_here * n_row
    cols_total = cols_here * n_col
    row_mod = Q * rows_total
    col_mod = Q * cols_total
    wave_matrix = realify(wave_form[:, 0], wave_form[:, 1])
    padded = extended(field, (("row", 0), ("col", 1)), 1)
    global_row = lax.axis_index("row") * rows_here + jnp.arange(rows_here, dtype=jnp.int32)
    global_col = lax.axis_index("col") * cols_here + jnp.arange(cols_here, dtype=jnp.int32)
    fine_row = (Q * global_row[:, None] + pillar_shift[:, :, 0]).reshape(-1)
    fine_col = (Q * global_col[None, :] + pillar_shift[:, :, 1]).reshape(-1)
    angles = wave_angle(wave_index, fine_row, fine_col, row_mod, col_mod)
    cos_all = jnp.cos(angles).T
    sin_all = jnp.sin(angles).T
    projected = jnp.dot(field.reshape(-1, width), wave_matrix, preferred_element_type=jnp.float32)
    projected = projected.reshape(rows_here * cols_here, sources, 2, waves)
    hi = lax.Precision.HIGHEST
    coeff_real = jnp.einsum("pw,psw->sw", cos_all, projected[:, :, 0], precision=hi) - jnp.einsum(
        "pw,psw->sw", sin_all, projected[:, :, 1], precision=hi
    )
    coeff_imag = jnp.einsum("pw,psw->sw", cos_all, projected[:, :, 1], precision=hi) + jnp.einsum(
        "pw,psw->sw", sin_all, projected[:, :, 0], precision=hi
    )
    partial_coeff = jnp.stack([coeff_real, coeff_imag], axis=1)
    near = jnp.zeros((rows_here, cols_here, sources, width), jnp.float32)
    for offset in range(9):
        step_row = offset // 3 - 1
        step_col = offset % 3 - 1
        block = padded[
            1 + step_row : 1 + step_row + rows_here, 1 + step_col : 1 + step_col + cols_here
        ]
        block = block.reshape(-1, width)
        for variant in range(near_kernel.shape[1]):
            near_mat = realify(near_kernel[offset, variant, 0], near_kernel[offset, variant, 1])
            product = jnp.dot(block, near_mat, preferred_element_type=jnp.float32).reshape(
                rows_here, cols_here, sources, width
            )
            chosen = (contact[:, :, offset] == variant)[:, :, None, None]
            near = near + jnp.where(chosen, product, jnp.float32(0.0))
    far_scale = math.sqrt(width // 2 / (waves * rows_total * cols_total))
    owned = lax.psum_scatter(partial_coeff, ("row", "col"), scatter_dimension=2, tiled=True)
    owner = lax.axis_index("row") * n_col + lax.axis_index("col")
    count = owned.shape[2]
    scales = far_scale * lax.dynamic_slice_in_dim(wave_weight, owner * owned.shape[2], count, 0)
    weighted = (scales[None, None, :] * owned).astype(jnp.bfloat16)
    add_weighted = lax.all_gather(weighted, ("row", "col"), axis=2, tiled=True)
    count = add_weighted.shape[2]
    cos_part = cos_all[:, None, :]
    sin_part = sin_all[:, None, :]
    weight_real = add_weighted[:, 0].astype(jnp.float32)[None]
    weight_imag = add_weighted[:, 1].astype(jnp.float32)[None]
    spread_real = cos_part * weight_real + sin_part * weight_imag
    spread_imag = cos_part * weight_imag - sin_part * weight_real
    spread = (
        jnp.concatenate([spread_real, spread_imag], axis=-1)
        .astype(jnp.bfloat16)
        .reshape(-1, 2 * count)
    )
    columns = jnp.concatenate(
        [
            lax.slice_in_dim(wave_matrix, 0, count, axis=1),
            lax.dynamic_slice_in_dim(wave_matrix, waves, count, 1),
        ],
        axis=1,
    )
    far = lax.dot_general(
        spread, columns, (((1,), (1,)), ((), ())), preferred_element_type=jnp.float32
    )
    return near + far.reshape(rows_here, cols_here, sources, width)


def solution(mesh):
    placed = (
        P("row", "col", None, None),
        P(),
        P("row", "col", None),
        P("row", "col", None),
        P(),
        P(),
        P(),
    )
    return jax.shard_map(
        local, mesh=mesh, in_specs=placed, out_specs=P("row", "col", None, None), check_vma=False
    )
```

profile of v0, /device:TPU:0, one launch (start us, length us, event | category | flops | bytes accessed | tf_op | source)
XLA Modules:
  0.0 1004.8 jit_solution(13671285341603411900)
XLA Ops:
  6.5 6.5 fusion.183
  13.0 5.8 copy.195
  18.8 2.6 copy.196
  22.5 7.4 convolution_bitcast_fusion
  29.9 8.9 copy.148
  38.8 11.8 %reshape.487 = f32[16,32,2,2048]{3,2,1,0:T(2,128)} reshape(f32[512,4096]{1,0:T(8,128)} %copy.148) | data formatting | bytes 16777216 | tf_op jit(solution)/shard_map/reshape | solution.py:68
  50.6 12.1 %fusion.180 = (f32[16,32,1,2048]{3,2,1,0:T(1,128)}, f32[16,32,1,2048]{3,2,1,0:T(1,128)}) fusion(f32[16,32,2,2048]{3,2,1,0:T(2,128)} %reshape.487), kind=kLoop, calls=%fused_computation.305 | loop fusion | bytes 16777216 | tf_op jit(solution)/shard_map/slice | solution.py:71
  64.9 6.9 fusion.6
  72.0 2.2 copy.149
  75.0 3.9 collective-permute-start.1
  78.9 2.7 fusion.181
  81.6 3.0 fusion.182
  84.6 1.7 fusion.178
  102.4 1.7 copy.218
  115.4 1.7 copy.204
  121.8 1.7 copy.200
  127.6 2.0 fusion.156
  129.6 2.6 fusion.83
  132.2 2.6 fusion.75
  145.6 1.7 copy.203
  147.2 1.7 copy.201
  152.1 1.9 compare_reduce_fusion.7
  156.9 6.8 collective-permute-start.3
  163.7 2.4 convolution_select_fusion
  166.1 2.5 convolution_select_fusion.1
  171.6 165.6 %all-reduce.3.cloned.1.call-done = f32[32,2,2048]{0,1,2:T(2,128)} async-done(((f32[32,2,2048]{0,1,2:T(2,128)}), f32[32,2,2048]{0,1,2:T(2,128)}) %all-reduce.3.cloned.1.call-update) | async-done | bytes 524304
  337.9 630.5 %all_gather.3 = bf16[32,2,2048]{0,1,2:T(2,128)(2,1)S(1)} all-gather(bf16[32,2,8]{0,1,2:T(2,128)(2,1)S(1)} %fusion.157), channel_id=1, replica_groups=mesh['row'=16,'col'=16] {'row','col'}, dimensions={2}, use_global_device_ids=true | all-gather | bytes 263168 | tf_op jit(solution)/shard_map/all_gather | solution.py:98
  968.4 2.2 slice_convert_fusion.1
  973.2 2.5 add_convert_fusion
  975.7 2.4 fusion
  993.3 1.9 fusion.26
  995.2 2.7 fusion.25
  (228 shorter events, 77.9 us)
Async XLA Ops:
  6.5 330.6 %all-reduce.3.cloned.1.call-start = ((), (), s32[]{:S(2)}) async-start(), calls=%async_computation | async-start | bytes 4194304
  50.6 12.7 %copy-start.57 = (s32[4,4,2]{1,2,0:T(2,128)S(1)}, s32[4,4,2]{1,2,0:T(2,128)}, u32[]{:S(2)}) copy-start(s32[4,4,2]{1,2,0:T(2,128)} %param.10) | copy-start | bytes 388
  50.6 13.6 %copy-start.56 = (s32[2048,2]{0,1:T(2,128)S(1)}, s32[2048,2]{0,1:T(2,128)}, u32[]{:S(2)}) copy-start(s32[2048,2]{0,1:T(2,128)} %param.11) | copy-start | bytes 49156
  64.1 7.8 copy-start.59
  75.0 79.0 %collective-permute-start = (bf16[1,4,32,512]{3,2,1,0:T(8,128)(2,1)}, bf16[1,4,32,512]{3,2,1,0:T(8,128)(2,1)}, u32[]{:S(2)}, u32[]{:S(2)}) collective-permute-start(bf16[1,4,32,512]{3,2,1,0:T(8,128)(2,1)} %get-tuple-element.89), channel_id=1, source_target_pairs={{0,16},{16,32},{32,48},{48,64},{64,80},{80,96},{96,112},{112,128},... | collective-permute-start | bytes 393224 | tf_op jit(solution)/shard_map/ppermute | solution.py:19
  75.0 80.1 %collective-permute-start.1 = (bf16[1,4,32,512]{3,2,1,0:T(8,128)(2,1)}, bf16[1,4,32,512]{3,2,1,0:T(8,128)(2,1)}, u32[]{:S(2)}, u32[]{:S(2)}) collective-permute-start(bf16[1,4,32,512]{3,2,1,0:T(8,128)(2,1)} %get-tuple-element.88), channel_id=1, source_target_pairs={{16,0},{32,16},{48,32},{64,48},{80,64},{96,80},{112,96},{128,112},... | collective-permute-start | bytes 393224 | tf_op jit(solution)/shard_map/ppermute | solution.py:21
  111.2 13.8 %copy-start.18 = (bf16[1,1,1,256,256]{3,4,2,1,0:T(8,128)(2,1)}, bf16[1,1,1,256,256]{3,4,2,1,0:T(8,128)(2,1)S(1)}, u32[]{:S(2)}) copy-start(bf16[1,1,1,256,256]{3,4,2,1,0:T(8,128)(2,1)S(1)} %copy.210) | copy-start | bytes 393220
  114.7 12.1 %copy-start.14 = (bf16[1,1,1,256,256]{3,4,2,1,0:T(8,128)(2,1)}, bf16[1,1,1,256,256]{3,4,2,1,0:T(8,128)(2,1)S(1)}, u32[]{:S(2)}) copy-start(bf16[1,1,1,256,256]{3,4,2,1,0:T(8,128)(2,1)S(1)} %copy.206) | copy-start | bytes 393220
  132.2 20.0 %copy-start.10 = (s32[4,4,9]{2,1,0:T(4,128)S(1)}, s32[4,4,9]{2,1,0:T(4,128)}, u32[]{:S(2)}) copy-start(s32[4,4,9]{2,1,0:T(4,128)} %param.9) | copy-start | bytes 1732
  140.8 22.9 %copy-start.53 = (bf16[1,1,1,256,256]{3,4,2,1,0:T(8,128)(2,1)S(1)}, bf16[1,1,1,256,256]{3,4,2,1,0:T(8,128)(2,1)}, u32[]{:S(2)}) copy-start(bf16[1,1,1,256,256]{3,4,2,1,0:T(8,128)(2,1)} %copy.223) | copy-start | bytes 393220
  147.2 18.9 %copy-start.27 = (bf16[1,1,1,256,256]{3,4,2,1,0:T(8,128)(2,1)S(1)}, bf16[1,1,1,256,256]{3,4,2,1,0:T(8,128)(2,1)}, u32[]{:S(2)}) copy-start(bf16[1,1,1,256,256]{3,4,2,1,0:T(8,128)(2,1)} %copy.222) | copy-start | bytes 393220
  147.2 18.9 %copy-start.44 = (bf16[256,256]{1,0:T(8,128)(2,1)S(1)}, bf16[256,256]{1,0:T(8,128)(2,1)}, u32[]{:S(2)}) copy-start(bf16[256,256]{1,0:T(8,128)(2,1)} %bitcast_negate_fusion.4) | copy-start | bytes 393220
  155.1 13.5 %copy-start.29 = (bf16[1,1,1,256,256]{3,4,2,1,0:T(8,128)(2,1)S(1)}, bf16[1,1,1,256,256]{3,4,2,1,0:T(8,128)(2,1)}, u32[]{:S(2)}) copy-start(bf16[1,1,1,256,256]{3,4,2,1,0:T(8,128)(2,1)} %copy.204) | copy-start | bytes 393220
  155.1 13.5 %copy-start.52 = (bf16[256,256]{1,0:T(8,128)(2,1)S(1)}, bf16[256,256]{1,0:T(8,128)(2,1)}, u32[]{:S(2)}) copy-start(bf16[256,256]{1,0:T(8,128)(2,1)} %bitcast_negate_fusion.13) | copy-start | bytes 393220
  155.2 13.5 %copy-start.55 = (bf16[1,1,1,256,256]{3,4,2,1,0:T(8,128)(2,1)S(1)}, bf16[1,1,1,256,256]{3,4,2,1,0:T(8,128)(2,1)}, u32[]{:S(2)}) copy-start(bf16[1,1,1,256,256]{3,4,2,1,0:T(8,128)(2,1)} %copy.203) | copy-start | bytes 393220
  156.9 821.2 %collective-permute-start.3 = (bf16[6,1,32,512]{3,2,1,0:T(8,128)(2,1)}, bf16[6,1,32,512]{3,2,1,0:T(8,128)(2,1)}, u32[]{:S(2)}, u32[]{:S(2)}) collective-permute-start(bf16[6,1,32,512]{3,2,1,0:T(8,128)(2,1)} %get-tuple-element.82), channel_id=1, source_target_pairs={{1,0},{2,1},{3,2},{4,3},{5,4},{6,5},{7,6},{8,7},{9,8},{10,9},{11,1... | collective-permute-start | bytes 589832 | tf_op jit(solution)/shard_map/ppermute | solution.py:21
  163.7 817.5 %collective-permute-start.2 = (bf16[6,1,32,512]{3,2,1,0:T(8,128)(2,1)}, bf16[6,1,32,512]{3,2,1,0:T(8,128)(2,1)}, u32[]{:S(2)}, u32[]{:S(2)}) collective-permute-start(bf16[6,1,32,512]{3,2,1,0:T(8,128)(2,1)} %get-tuple-element.81), channel_id=1, source_target_pairs={{0,1},{1,2},{2,3},{3,4},{4,5},{5,6},{6,7},{7,8},{8,9},{9,10},{10,1... | collective-permute-start | bytes 589832 | tf_op jit(solution)/shard_map/ppermute | solution.py:19
  166.1 4.0 copy-start.28
  166.1 4.0 copy-start.50
  166.1 4.0 copy-start.54
  978.2 3.0 copy-start.25
  978.2 3.0 copy-start.38
  978.2 3.0 copy-start.48
  978.2 3.0 copy-start.67
  979.8 3.0 copy-start.23
  979.8 3.0 copy-start.36
  979.8 3.0 copy-start.47
  979.8 3.0 copy-start.66
  988.8 3.1 copy-start.20
  988.8 3.1 copy-start.33
  988.8 3.1 copy-start.41
  988.8 3.1 copy-start.60
  (43 other events, 108.7 us)
Sparse Core Ops, SparseCore 0:
  74.4 262.6 all-reduce.2
where the time goes:
time: 1010 us; the launch traced here: 1000 us
  blocking collectives  630 us (62%)
  waiting for transfers between devices  166 us (16%)
  local copies, waits for them, and re-layouts  102 us (10%)
  matrix products  41.5 us (4%)
  other arithmetic  40.3 us (4%)
  between operations  14.6 us (1%)
  starting transfers between devices  10.6 us (1%)
    all_gather x1, blocking collectives, local(): add_weighted = lax.all_gather(weighted, ('row', 'col'), axis=2, tiled=True)  630 us
    unnamed x2, waiting for transfers between devices  166 us
    unnamed x175, local copies, waits for them, and re-layouts  48.2 us
    dot_general x18, matrix products, local(): jnp.dot(block, near_mat, preferred_element_type=jnp.float32)  31.8 us
    neg x18, other arithmetic, realify(): lower = jnp.concatenate([-imag_part.T, real_part.T], axis=1)  21.7 us
  transfers between devices with their start and end apart: 5, of which 1 were waited for; matrix products, arithmetic and copies ran while one was open for 10% of the time, Pallas kernels for 0%

commit v1 on v0

--- a/solution.py
+++ b/solution.py
@@ -95,7 +95,15 @@
     count = owned.shape[2]
     scales = far_scale * lax.dynamic_slice_in_dim(wave_weight, owner * owned.shape[2], count, 0)
     weighted = (scales[None, None, :] * owned).astype(jnp.bfloat16)
-    add_weighted = lax.all_gather(weighted, ("row", "col"), axis=2, tiled=True)
+    add_weighted = jnp.concatenate(
+        lax.all_to_all(
+            jnp.stack([weighted for _ in range(lax.psum(1, axis_name=("row", "col")))], 0),
+            axis_name=("row", "col"),
+            concat_axis=0,
+            split_axis=0,
+        ),
+        2,
+    )
     count = add_weighted.shape[2]
     cos_part = cos_all[:, None, :]
     sin_part = sin_all[:, None, :]

time: 1010 us -> 395 us (0.39)
  blocking collectives: 630 us -> 0 us
  starting transfers between devices: 10.6 us -> 22.9 us
  waiting for transfers between devices: 166 us -> 178 us
    all_gather x1 -> x0, blocking collectives: 630 us -> none  [local(): add_weighted = lax.all_gather(weighted, ('row', 'col'), axis=2, tiled=True)]
    unnamed x2, waiting for transfers between devices: 166 us -> 178 us
    all_to_all x0 -> x1, starting transfers between devices: none -> 12.3 us  [local(): lax.all_to_all(jnp.stack([weighted for _ in range(lax.psum(1, axis_name=(...]
    unnamed x175 -> x165, local copies, waits for them, and re-layouts: 48.2 us -> 43.1 us
  transfers between devices with their start and end apart: 5 -> 6, of which waited for: 1 -> 1; matrix products, arithmetic and copies ran while one was open for 10% -> 25% of each run, Pallas kernels for 0% -> 0%
where the time goes in v1:
time: 395 us; the launch traced here: 393 us
  waiting for transfers between devices  178 us (45%)
  local copies, waits for them, and re-layouts  95.7 us (24%)
  matrix products  44.3 us (11%)
  other arithmetic  37.2 us (9%)
  starting transfers between devices  22.9 us (6%)
  between operations  14.3 us (4%)
    unnamed x2, waiting for transfers between devices  178 us
    unnamed x165, local copies, waits for them, and re-layouts  43.1 us
    dot_general x18, matrix products, local(): jnp.dot(block, near_mat, preferred_element_type=jnp.float32)  34.6 us
    neg x18, other arithmetic, realify(): lower = jnp.concatenate([-imag_part.T, real_part.T], axis=1)  21 us
    all_to_all x1, starting transfers between devices, local(): lax.all_to_all(jnp.stack([weighted for _ in range(lax.psum(1, axis_name=(...  12.3 us
    slice x1, local copies, waits for them, and re-layouts, local(): projected[:, :, 1]  12.2 us
    reshape x1, local copies, waits for them, and re-layouts, local(): projected = projected.reshape(rows_here * cols_here, sources, 2, waves)  11.8 us
    ppermute x2, starting transfers between devices, extended(): lax.ppermute(head, axis, [((i + 1) % count, i) for i in range(count)])  10.6 us
  transfers between devices with their start and end apart: 6, of which 1 were waited for; matrix products, arithmetic and copies ran while one was open for 25% of the time, Pallas kernels for 0%

profile of v1, /device:TPU:0, one launch (start us, length us, event | category | flops | bytes accessed | tf_op | source)
XLA Modules:
  0.0 392.7 jit_solution(6565594236976592255)
XLA Ops:
  6.5 6.5 %fusion.185 = (bf16[2048,1,256]{2,1,0:T(2,128)(2,1)S(1)}, bf16[2048,1,256]{2,1,0:T(2,128)(2,1)}) fusion(bf16[2048,2,256]{2,1,0:T(2,128)(2,1)} %param.12), kind=kLoop, calls=%fused_computation.312 | loop fusion | bytes 4194304 | tf_op jit(solution)/shard_map/slice | solution.py:58
  13.0 5.8 %copy.241 = bf16[2048,1,256]{0,2,1:T(8,128)(2,1)} copy(bf16[2048,1,256]{2,1,0:T(2,128)(2,1)} %get-tuple-element.78) | data formatting | bytes 2097152
  18.8 2.6 copy.242
  22.6 7.4 %convolution_bitcast_fusion = f32[512,4096]{0,1:T(8,128)} fusion(bf16[512,512]{1,0:T(8,128)(2,1)} %bitcast.302, bf16[256,2048]{1,0:T(8,128)(2,1)} %bitcast.305, bf16[256,2048]{1,0:T(8,128)(2,1)S(1)} %bitcast_negate_fusion, bf16[256,2048]{1,0:T(8,128)(2,1)S(1)} %bitcast.298), kind=kOutput, calls=%fused_computation | convolution fusion | flops 2164260864 | bytes 12058624 | tf_op jit(solution)/shard_map/dot_general | solution.py:67
  30.0 9.0 %copy.192 = f32[512,4096]{1,0:T(8,128)} copy(f32[512,4096]{0,1:T(8,128)} %convolution_bitcast_fusion) | data formatting | bytes 16777216 | tf_op jit(solution)/shard_map/dot_general | solution.py:67
  38.9 11.8 %reshape.495 = f32[16,32,2,2048]{3,2,1,0:T(2,128)} reshape(f32[512,4096]{1,0:T(8,128)} %copy.192) | data formatting | bytes 16777216 | tf_op jit(solution)/shard_map/reshape | solution.py:68
  50.7 12.2 %fusion.182 = (f32[16,32,1,2048]{3,2,1,0:T(1,128)}, f32[16,32,1,2048]{3,2,1,0:T(1,128)}) fusion(f32[16,32,2,2048]{3,2,1,0:T(2,128)} %reshape.495), kind=kLoop, calls=%fused_computation.309 | loop fusion | bytes 16777216 | tf_op jit(solution)/shard_map/slice | solution.py:71
  65.8 6.9 %fusion.6 = (f32[2048,32]{0,1:T(8,128)S(1)}, f32[2048,32]{0,1:T(8,128)S(1)}, f32[2048,32]{0,1:T(8,128)S(1)}, f32[2048,32]{0,1:T(8,128)S(1)}) fusion(f32[16,32,1,2048]{3,2,1,0:T(1,128)} %get-tuple-element.38, f32[2048,16]{0,1:T(8,128)S(1)} %get-tuple-element.97, f32[2048,16]{0,1:T(8,128)S(1)} %get-tuple-element.96, f32[16,32,1,2048]{3,2,1,0:T(1,128)} %get-tuple-element.37), kind=kLoop, calls=%fused_computation.12 | loop fusion | flops 8126464 | bytes 9699328 | tf_op jit(solution)/shard_map/pw,psw->sw/dot_general | solution.py:70
  72.8 2.3 copy.193
  75.9 3.9 collective-permute-start.1
  79.7 2.7 fusion.183
  82.4 2.7 fusion.184
  85.1 1.7 fusion.180
  86.8 1.7 copy.274
  93.3 1.7 copy.270
  96.5 1.7 copy.268
  103.0 1.7 copy.264
  124.1 2.0 fusion.158
  126.1 2.5 fusion.85
  128.6 2.6 fusion.77
  147.1 6.7 %collective-permute-start.3 = (bf16[6,1,32,512]{3,2,1,0:T(8,128)(2,1)}, bf16[6,1,32,512]{3,2,1,0:T(8,128)(2,1)}, u32[]{:S(2)}, u32[]{:S(2)}) collective-permute-start(bf16[6,1,32,512]{3,2,1,0:T(8,128)(2,1)} %get-tuple-element.82), channel_id=1, source_target_pairs={{1,0},{2,1},{3,2},{4,3},{5,4},{6,5},{7,6},{8,7},{9,8},{10,9},{11,1... | collective-permute-start | bytes 589832 | tf_op jit(solution)/shard_map/ppermute | solution.py:21
  159.7 178.2 %all-reduce.3.cloned.1.call-done = f32[32,2,2048]{0,1,2:T(2,128)} async-done(((f32[32,2,2048]{0,1,2:T(2,128)}), f32[32,2,2048]{0,1,2:T(2,128)}) %all-reduce.3.cloned.1.call-update) | async-done | bytes 524304
  340.2 12.3 %all-to-all-start = ((bf16[256,2,256]{2,1,0:T(2,128)(2,1)}), bf16[256,2,256]{2,1,0:T(2,128)(2,1)S(1)}, u32[]{:S(2)}, u32[]{:S(2)}) async-start(bf16[256,2,256]{2,1,0:T(2,128)(2,1)} %reshape.555), calls=%async_computation | async-start | bytes 524288 | tf_op jit(solution)/shard_map/all_to_all | solution.py:99
  352.6 2.6 convolution_select_fusion.4
  355.2 2.6 convolution_select_fusion.5
  357.8 2.4 convolution_select_fusion.6
  360.2 2.4 convolution_select_fusion.7
  362.7 2.4 convolution_select_fusion.8
  372.4 1.7 fusion.26
  377.7 2.4 add_convert_fusion
  380.3 2.4 fusion
  383.3 2.6 fusion.25
  (220 shorter events, 70.5 us)
Async XLA Ops:
  6.5 331.4 %all-reduce.3.cloned.1.call-start = ((), (), s32[]{:S(2)}) async-start(), calls=%async_computation.1 | async-start | bytes 4194304
  21.5 8.5 %copy-start = (bf16[2048,1,256]{0,2,1:T(8,128)(2,1)}, bf16[2048,1,256]{0,2,1:T(8,128)(2,1)S(1)}, u32[]{:S(2)}) copy-start(bf16[2048,1,256]{0,2,1:T(8,128)(2,1)S(1)} %copy.242) | copy-start | bytes 3145732
  50.7 12.9 %copy-start.60 = (s32[4,4,2]{1,2,0:T(2,128)S(1)}, s32[4,4,2]{1,2,0:T(2,128)}, u32[]{:S(2)}) copy-start(s32[4,4,2]{1,2,0:T(2,128)} %param.10) | copy-start | bytes 388
  50.7 14.3 %copy-start.59 = (s32[2048,2]{0,1:T(2,128)S(1)}, s32[2048,2]{0,1:T(2,128)}, u32[]{:S(2)}) copy-start(s32[2048,2]{0,1:T(2,128)} %param.11) | copy-start | bytes 49156
  75.9 68.4 %collective-permute-start = (bf16[1,4,32,512]{3,2,1,0:T(8,128)(2,1)}, bf16[1,4,32,512]{3,2,1,0:T(8,128)(2,1)}, u32[]{:S(2)}, u32[]{:S(2)}) collective-permute-start(bf16[1,4,32,512]{3,2,1,0:T(8,128)(2,1)} %get-tuple-element.89), channel_id=1, source_target_pairs={{0,16},{16,32},{32,48},{48,64},{64,80},{80,96},{96,112},{112,128},... | collective-permute-start | bytes 393224 | tf_op jit(solution)/shard_map/ppermute | solution.py:19
  75.9 69.5 %collective-permute-start.1 = (bf16[1,4,32,512]{3,2,1,0:T(8,128)(2,1)}, bf16[1,4,32,512]{3,2,1,0:T(8,128)(2,1)}, u32[]{:S(2)}, u32[]{:S(2)}) collective-permute-start(bf16[1,4,32,512]{3,2,1,0:T(8,128)(2,1)} %get-tuple-element.88), channel_id=1, source_target_pairs={{16,0},{32,16},{48,32},{64,48},{80,64},{96,80},{112,96},{128,112},... | collective-permute-start | bytes 393224 | tf_op jit(solution)/shard_map/ppermute | solution.py:21
  109.5 13.1 %copy-start.22 = (bf16[1,1,1,256,256]{3,4,2,1,0:T(8,128)(2,1)}, bf16[1,1,1,256,256]{3,4,2,1,0:T(8,128)(2,1)S(1)}, u32[]{:S(2)}) copy-start(bf16[1,1,1,256,256]{3,4,2,1,0:T(8,128)(2,1)S(1)} %copy.256) | copy-start | bytes 393220
  111.2 11.2 %copy-start.20 = (bf16[1,1,1,256,256]{3,4,2,1,0:T(8,128)(2,1)}, bf16[1,1,1,256,256]{3,4,2,1,0:T(8,128)(2,1)S(1)}, u32[]{:S(2)}) copy-start(bf16[1,1,1,256,256]{3,4,2,1,0:T(8,128)(2,1)S(1)} %copy.254) | copy-start | bytes 393220
  128.6 14.2 %copy-start.17 = (s32[4,4,9]{2,1,0:T(4,128)S(1)}, s32[4,4,9]{2,1,0:T(4,128)}, u32[]{:S(2)}) copy-start(s32[4,4,9]{2,1,0:T(4,128)} %param.9) | copy-start | bytes 1732
  131.2 22.6 %copy-start.33 = (bf16[1,1,1,256,256]{3,4,2,1,0:T(8,128)(2,1)S(1)}, bf16[1,1,1,256,256]{3,4,2,1,0:T(8,128)(2,1)}, u32[]{:S(2)}) copy-start(bf16[1,1,1,256,256]{3,4,2,1,0:T(8,128)(2,1)} %copy.270) | copy-start | bytes 393220
  131.2 22.6 %copy-start.45 = (bf16[256,256]{1,0:T(8,128)(2,1)S(1)}, bf16[256,256]{1,0:T(8,128)(2,1)}, u32[]{:S(2)}) copy-start(bf16[256,256]{1,0:T(8,128)(2,1)} %bitcast_negate_fusion.3) | copy-start | bytes 393220
  134.3 19.6 %copy-start.57 = (bf16[1,1,1,256,256]{3,4,2,1,0:T(8,128)(2,1)S(1)}, bf16[1,1,1,256,256]{3,4,2,1,0:T(8,128)(2,1)}, u32[]{:S(2)}) copy-start(bf16[1,1,1,256,256]{3,4,2,1,0:T(8,128)(2,1)} %copy.269) | copy-start | bytes 393220
  141.1 14.2 %copy-start.32 = (bf16[1,1,1,256,256]{3,4,2,1,0:T(8,128)(2,1)S(1)}, bf16[1,1,1,256,256]{3,4,2,1,0:T(8,128)(2,1)}, u32[]{:S(2)}) copy-start(bf16[1,1,1,256,256]{3,4,2,1,0:T(8,128)(2,1)} %copy.268) | copy-start | bytes 393220
  141.1 14.2 %copy-start.44 = (bf16[256,256]{1,0:T(8,128)(2,1)S(1)}, bf16[256,256]{1,0:T(8,128)(2,1)}, u32[]{:S(2)}) copy-start(bf16[256,256]{1,0:T(8,128)(2,1)} %bitcast_negate_fusion.4) | copy-start | bytes 393220
  141.1 14.2 %copy-start.56 = (bf16[1,1,1,256,256]{3,4,2,1,0:T(8,128)(2,1)S(1)}, bf16[1,1,1,256,256]{3,4,2,1,0:T(8,128)(2,1)}, u32[]{:S(2)}) copy-start(bf16[1,1,1,256,256]{3,4,2,1,0:T(8,128)(2,1)} %copy.267) | copy-start | bytes 393220
  145.4 11.4 %copy-start.35 = (bf16[1,1,1,256,256]{3,4,2,1,0:T(8,128)(2,1)S(1)}, bf16[1,1,1,256,256]{3,4,2,1,0:T(8,128)(2,1)}, u32[]{:S(2)}) copy-start(bf16[1,1,1,256,256]{3,4,2,1,0:T(8,128)(2,1)} %copy.250) | copy-start | bytes 393220
  145.4 11.4 %copy-start.52 = (bf16[256,256]{1,0:T(8,128)(2,1)S(1)}, bf16[256,256]{1,0:T(8,128)(2,1)}, u32[]{:S(2)}) copy-start(bf16[256,256]{1,0:T(8,128)(2,1)} %bitcast_negate_fusion.13) | copy-start | bytes 393220
  145.4 11.4 %copy-start.58 = (bf16[1,1,1,256,256]{3,4,2,1,0:T(8,128)(2,1)S(1)}, bf16[1,1,1,256,256]{3,4,2,1,0:T(8,128)(2,1)}, u32[]{:S(2)}) copy-start(bf16[1,1,1,256,256]{3,4,2,1,0:T(8,128)(2,1)} %copy.249) | copy-start | bytes 393220
  147.1 205.4 %collective-permute-start.3 = (bf16[6,1,32,512]{3,2,1,0:T(8,128)(2,1)}, bf16[6,1,32,512]{3,2,1,0:T(8,128)(2,1)}, u32[]{:S(2)}, u32[]{:S(2)}) collective-permute-start(bf16[6,1,32,512]{3,2,1,0:T(8,128)(2,1)} %get-tuple-element.82), channel_id=1, source_target_pairs={{1,0},{2,1},{3,2},{4,3},{5,4},{6,5},{7,6},{8,7},{9,8},{10,9},{11,1... | collective-permute-start | bytes 589832 | tf_op jit(solution)/shard_map/ppermute | solution.py:21
  153.8 203.9 %collective-permute-start.2 = (bf16[6,1,32,512]{3,2,1,0:T(8,128)(2,1)S(1)}, bf16[6,1,32,512]{3,2,1,0:T(8,128)(2,1)}, u32[]{:S(2)}, u32[]{:S(2)}) collective-permute-start(bf16[6,1,32,512]{3,2,1,0:T(8,128)(2,1)S(1)} %get-tuple-element.81), channel_id=1, source_target_pairs={{0,1},{1,2},{2,3},{3,4},{4,5},{5,6},{6,7},{7,8},{8,9},{9,10},{10,1... | collective-permute-start | bytes 589832 | tf_op jit(solution)/shard_map/ppermute | solution.py:19
  156.8 195.7 %copy-start.31 = (bf16[1,1,1,256,256]{3,4,2,1,0:T(8,128)(2,1)S(1)}, bf16[1,1,1,256,256]{3,4,2,1,0:T(8,128)(2,1)}, u32[]{:S(2)}) copy-start(bf16[1,1,1,256,256]{3,4,2,1,0:T(8,128)(2,1)} %copy.274) | copy-start | bytes 393220
  159.7 195.4 %copy-start.29 = (bf16[1,1,1,256,256]{3,4,2,1,0:T(8,128)(2,1)S(1)}, bf16[1,1,1,256,256]{3,4,2,1,0:T(8,128)(2,1)}, u32[]{:S(2)}) copy-start(bf16[1,1,1,256,256]{3,4,2,1,0:T(8,128)(2,1)} %copy.272) | copy-start | bytes 393220
  340.2 33.9 %all-to-all-start = ((bf16[256,2,256]{2,1,0:T(2,128)(2,1)}), bf16[256,2,256]{2,1,0:T(2,128)(2,1)S(1)}, u32[]{:S(2)}, u32[]{:S(2)}) async-start(bf16[256,2,256]{2,1,0:T(2,128)(2,1)} %reshape.555), calls=%async_computation | async-start | bytes 524288 | tf_op jit(solution)/shard_map/all_to_all | solution.py:99
  352.5 5.2 %copy-start.30 = (bf16[1,1,1,256,256]{3,4,2,1,0:T(8,128)(2,1)S(1)}, bf16[1,1,1,256,256]{3,4,2,1,0:T(8,128)(2,1)}, u32[]{:S(2)}) copy-start(bf16[1,1,1,256,256]{3,4,2,1,0:T(8,128)(2,1)} %copy.266) | copy-start | bytes 393220
  352.6 5.2 %copy-start.43 = (bf16[256,256]{1,0:T(8,128)(2,1)S(1)}, bf16[256,256]{1,0:T(8,128)(2,1)}, u32[]{:S(2)}) copy-start(bf16[256,256]{1,0:T(8,128)(2,1)} %bitcast_negate_fusion.5) | copy-start | bytes 393220
  352.6 5.2 %copy-start.55 = (bf16[1,1,1,256,256]{3,4,2,1,0:T(8,128)(2,1)S(1)}, bf16[1,1,1,256,256]{3,4,2,1,0:T(8,128)(2,1)}, u32[]{:S(2)}) copy-start(bf16[1,1,1,256,256]{3,4,2,1,0:T(8,128)(2,1)} %copy.265) | copy-start | bytes 393220
  355.1 5.0 %copy-start.28 = (bf16[1,1,1,256,256]{3,4,2,1,0:T(8,128)(2,1)S(1)}, bf16[1,1,1,256,256]{3,4,2,1,0:T(8,128)(2,1)}, u32[]{:S(2)}) copy-start(bf16[1,1,1,256,256]{3,4,2,1,0:T(8,128)(2,1)} %copy.264) | copy-start | bytes 393220
  355.2 5.0 %copy-start.42 = (bf16[256,256]{1,0:T(8,128)(2,1)S(1)}, bf16[256,256]{1,0:T(8,128)(2,1)}, u32[]{:S(2)}) copy-start(bf16[256,256]{1,0:T(8,128)(2,1)} %bitcast_negate_fusion.6) | copy-start | bytes 393220
  355.2 5.0 %copy-start.54 = (bf16[1,1,1,256,256]{3,4,2,1,0:T(8,128)(2,1)S(1)}, bf16[1,1,1,256,256]{3,4,2,1,0:T(8,128)(2,1)}, u32[]{:S(2)}) copy-start(bf16[1,1,1,256,256]{3,4,2,1,0:T(8,128)(2,1)} %copy.263) | copy-start | bytes 393220
  357.8 4.8 %copy-start.27 = (bf16[1,1,1,256,256]{3,4,2,1,0:T(8,128)(2,1)S(1)}, bf16[1,1,1,256,256]{3,4,2,1,0:T(8,128)(2,1)}, u32[]{:S(2)}) copy-start(bf16[1,1,1,256,256]{3,4,2,1,0:T(8,128)(2,1)} %copy.262) | copy-start | bytes 393220
  360.2 4.9 %copy-start.26 = (bf16[1,1,1,256,256]{3,4,2,1,0:T(8,128)(2,1)S(1)}, bf16[1,1,1,256,256]{3,4,2,1,0:T(8,128)(2,1)}, u32[]{:S(2)}) copy-start(bf16[1,1,1,256,256]{3,4,2,1,0:T(8,128)(2,1)} %copy-done.25) | copy-start | bytes 393220
  360.2 4.8 %copy-start.40 = (bf16[256,256]{1,0:T(8,128)(2,1)S(1)}, bf16[256,256]{1,0:T(8,128)(2,1)}, u32[]{:S(2)}) copy-start(bf16[256,256]{1,0:T(8,128)(2,1)} %bitcast_negate_fusion.9) | copy-start | bytes 393220
  (37 other events, 106.7 us)
Sparse Core Ops, SparseCore 0:
  75.3 262.6 all-reduce.2
